TPU v7x, 128 devices: a whole 4x4x4 slice. The times are simulated.
128 devices in a mesh: blk: 4 (over x), tok: 32 (over y, z, core).
Axes of the slice: x: 4, y: 4, z: 4, core: 2. Of those that a mesh axis runs over, the one named last changes fastest.
Arguments:
- tokens: bfloat16 [32, 1024, 1664], P('tok', 'blk'), may hold values from -6 to 6
- segment_ids: int32 [32, 1024], P('tok'), may hold values from 0 to 31, as said below
- merge_index: int32 [32, 256, 4], P('tok'), may hold values from 0 to 1023, as said below
- segment_owner: int32 [32, 32], P('tok'), may hold values from 0 to 31, each once within a row
- ln1_gain: float32 [1664], replicated, may hold values from 0.1 to 1.9
- ln1_bias: float32 [1664], replicated, may hold values from -4 to 4
- w_qkv: bfloat16 [3, 1664, 1664], P(None, 'tok', 'blk'), may hold values from -0.15625 to 0.15625
- qkv_bias: float32 [3, 1664], P(None, 'blk'), may hold values from -6 to 6
- w_out: bfloat16 [1664, 1664], P('blk', 'tok'), may hold values from -0.15625 to 0.15625
- out_bias: float32 [1664], replicated, may hold values from -6 to 6
- ln2_gain: float32 [1664], replicated, may hold values from 0.1 to 1.9
- ln2_bias: float32 [1664], replicated, may hold values from -4 to 4
- w_fc1: bfloat16 [1664, 8192], P(None, 'blk'), may hold values from -0.15625 to 0.15625
- fc1_bias: float32 [8192], P('blk'), may hold values from -6 to 6
- w_fc2: bfloat16 [8192, 1664], P('blk'), may hold values from -0.0625 to 0.0625
- fc2_bias: float32 [1664], replicated, may hold values from -6 to 6
- ln3_gain: float32 [1664], replicated, may hold values from 0.1 to 1.9
- ln3_bias: float32 [1664], replicated, may hold values from -4 to 4
- w_proj: bfloat16 [6656, 1664], P('tok', 'blk'), may hold values from -0.078125 to 0.078125
- proj_bias: float32 [1664], P('blk'), may hold values from -6 to 6
Outputs:
- returned: bfloat16 [32, 32, 16, 1664], P('tok', None, None, 'blk')
Inputs may be any that keep to these rules, and one draw needn't show every extreme that they name: `segment_ids`: within a block each segment holds 4 to 64 tokens, one exactly 64; the four tokens of one row of merge_index share a segment. `merge_index`: the rows of one block name each token of the block exactly once. `segment_owner`: each block's row is a permutation of the owners.
All inputs are finite; a program needn't handle non-finite values.
Results may differ from a plain program's by a relative error of at most 0.015.
Values may be sent and summed in bfloat16 or wider, within the bound.
A program may use at most 128 MiB of HBM per device.

v0:
```python
import math
import jax
import jax.numpy as jnp
from jax import lax
from jax.sharding import PartitionSpec as P

HD = 104
EPS = 1e-06


def layer_norm(input_tensors, scales, offset):
    input_tensors = input_tensors.astype(jnp.float32)
    center = input_tensors - jnp.mean(input_tensors, axis=-1, keepdims=True)
    spread = jnp.mean(center * center, axis=-1, keepdims=True)
    return center * lax.rsqrt(spread + EPS) * scales + offset


def body(
    tokens,
    segment_ids,
    merge_index,
    segment_owner,
    ln1_gain,
    ln1_bias,
    w_qkv,
    qkv_bias,
    w_out,
    out_bias,
    ln2_gain,
    ln2_bias,
    w_fc1,
    fc1_bias,
    w_fc2,
    fc2_bias,
    ln3_gain,
    ln3_bias,
    w_proj,
    proj_bias,
):
    tok_block = tokens[0]
    row_count = tok_block.shape[0]
    model_width = tok_block.shape[1]
    head_cols = w_qkv.shape[2]
    heads_here = head_cols // HD
    normed_one = layer_norm(tok_block, ln1_gain, ln1_bias).astype(jnp.bfloat16)
    normed_all = lax.all_gather(normed_one, "blk", axis=0, tiled=True)
    all_rows = normed_all.shape[0]
    columns = normed_all
    projected_qkv = jnp.einsum(
        "td,cde->cte",
        columns,
        lax.all_gather(w_qkv, "tok", axis=1, tiled=True),
        preferred_element_type=jnp.float32,
    )
    projected_qkv = (projected_qkv + qkv_bias[:, None, :]).astype(jnp.bfloat16)
    projected_qkv = projected_qkv.reshape(3, all_rows, heads_here, HD)
    key_rows = projected_qkv[1]
    values = projected_qkv[2]
    segment_row = segment_ids[0]
    q_block = min(512, all_rows)
    block_count = all_rows // q_block
    query_rows = projected_qkv[0].reshape(block_count, q_block, heads_here, HD)
    query_segs = segment_row.reshape(block_count, q_block)
    score_scale = 1.0 / math.sqrt(HD)

    def attend(input_tensors):
        query_part, query_seg = input_tensors
        scores = (
            jnp.einsum("qhe,khe->hqk", query_part, key_rows, preferred_element_type=jnp.float32)
            * score_scale
        )
        allowed = query_seg[:, None] == segment_row[None, :]
        weights = jnp.where(allowed[None], jnp.exp(scores), 0.0)
        attn_probs = (weights / jnp.sum(weights, axis=-1, keepdims=True)).astype(jnp.bfloat16)
        mixed = jnp.einsum("hqk,khe->qhe", attn_probs, values, preferred_element_type=jnp.float32)
        return mixed.astype(jnp.bfloat16)

    attended = lax.map(attend, (query_rows, query_segs)).reshape(all_rows, head_cols)
    out_full = lax.all_gather(w_out, "tok", axis=1, tiled=True)
    attn_rows = lax.psum_scatter(
        jnp.dot(attended, out_full, preferred_element_type=jnp.float32).astype(jnp.bfloat16),
        "blk",
        scatter_dimension=0,
        tiled=True,
    ).astype(jnp.float32)
    after_attn = tok_block.astype(jnp.float32) + attn_rows + out_bias
    normed_two = layer_norm(after_attn, ln2_gain, ln2_bias).astype(jnp.bfloat16)
    pre_act = (
        jnp.dot(
            lax.all_gather(normed_two, "blk", axis=0, tiled=True),
            w_fc1,
            preferred_element_type=jnp.float32,
        )
        + fc1_bias
    )
    hidden_act = jax.nn.gelu(pre_act, approximate=False).astype(jnp.bfloat16)
    partial_sum = jnp.dot(hidden_act, w_fc2, preferred_element_type=jnp.float32)
    own_start = lax.axis_index("blk") * row_count
    own_rows = lax.dynamic_slice_in_dim(partial_sum, own_start, row_count, 0) + after_attn
    partial_sum = lax.dynamic_update_slice_in_dim(partial_sum, own_rows, own_start, 0)
    summed = lax.psum(partial_sum.astype(jnp.bfloat16), "blk").astype(jnp.float32)
    layer_all = (summed + fc2_bias).astype(jnp.bfloat16)
    final_all = layer_norm(layer_all, ln3_gain, ln3_bias).astype(jnp.bfloat16)
    merge_rows = merge_index[0]
    merged_count = merge_rows.shape[0]
    merged = jnp.take(final_all, merge_rows.reshape(-1), axis=0).reshape(
        merged_count, 4 * model_width
    )
    columns = merged
    projected = jnp.dot(
        columns,
        lax.all_gather(w_proj, "tok", axis=0, tiled=True),
        preferred_element_type=jnp.float32,
    )
    projected = (projected + proj_bias).astype(jnp.bfloat16)
    tok_count = lax.axis_size("tok")
    slot_cap = 2 * merged_count // tok_count
    owners_here = segment_owner[0]
    seg_rows = jnp.take(segment_row, merge_rows[:, 0])
    seg_match = (
        seg_rows[:, None] == jnp.arange(owners_here.shape[0], dtype=jnp.int32)[None, :]
    ).astype(jnp.int32)
    owner_rows = jnp.sum(seg_match * owners_here[None, :], axis=1)
    segment_matches = (
        owner_rows[:, None] == jnp.arange(tok_count, dtype=jnp.int32)[None, :]
    ).astype(jnp.int32)
    before = jnp.cumsum(segment_matches, axis=0) - segment_matches
    order_in = jnp.sum(before * segment_matches, axis=1)
    target = owner_rows * slot_cap + order_in
    placed = (jnp.arange(tok_count * slot_cap, dtype=jnp.int32)[:, None] == target[None, :]).astype(
        jnp.bfloat16
    )
    outgoing = jnp.dot(placed, projected, preferred_element_type=jnp.float32).astype(jnp.bfloat16)
    outgoing = outgoing.reshape(tok_count, slot_cap, projected.shape[1])
    arrived = lax.all_to_all(outgoing, "tok", split_axis=0, concat_axis=0, tiled=True)
    return arrived[None]


def solution(mesh):
    placed = (
        P("tok", "blk", None),
        P("tok", None),
        P("tok", None, None),
        P("tok", None),
        P(),
        P(),
        P(None, "tok", "blk"),
        P(None, "blk"),
        P("blk", "tok"),
        P(),
        P(),
        P(),
        P(None, "blk"),
        P("blk"),
        P("blk", None),
        P(),
        P(),
        P(),
        P("tok", "blk"),
        P("blk"),
    )
    return jax.shard_map(
        body, mesh=mesh, in_specs=placed, out_specs=P("tok", None, None, "blk"), check_vma=False
    )
```

profile of v0, /device:TPU:1, one launch (start us, length us, event | category | flops | bytes accessed | tf_op | source)
XLA Modules:
  0.0 480.8 jit_solution(5821261523930769322)
XLA Ops:
  6.5 0.7 all-gather.15.cloned.1.call-update
  7.3 0.0 all-gather.7.cloned.1.call-start
  7.3 1.3 convert_reduce_fusion.1
  8.7 1.5 fusion.43
  10.2 2.5 fusion.46
  12.8 0.0 all-gather.9.cloned.1.call-start
  12.8 1.7 copy.32
  14.5 0.0 reduce-scatter.2.cloned.1.call-start
  14.6 0.5 broadcast.197
  15.1 1.3 reduce.6
  16.4 40.5 %all-gather.15.cloned.1.call-done = bf16[32,52,416]{2,1,0:T(8,128)(2,1)} async-done(((bf16[1,52,416]{2,1,0:T(8,128)(2,1)}), bf16[32,52,416]{2,1,0:T(8,128)(2,1)}) %all-gather.15.cloned.1.call-update) | async-done | bytes 1384464 | tf_op jit(solution)/shard_map/all_gather | solution.py:79
  56.9 2.7 reshape.179
  59.7 39.4 %all-gather.7.cloned.1.call-done = bf16[1024,1664]{1,0:T(8,128)(2,1)} async-done(((bf16[256,1664]{1,0:T(8,128)(2,1)}), bf16[1024,1664]{1,0:T(8,128)(2,1)}) %all-gather.7.cloned.1.call-update) | async-done | bytes 3407888 | tf_op jit(solution)/shard_map/all_gather | solution.py:46
  99.1 53.1 %all-gather.9.cloned.1.call-done = bf16[3,1664,416]{2,0,1:T(4,128)(2,1)} async-done(((bf16[3,52,416]{2,0,1:T(4,128)(2,1)}), bf16[3,1664,416]{2,0,1:T(4,128)(2,1)}) %all-gather.9.cloned.1.call-update) | async-done | bytes 4153360 | tf_op jit(solution)/shard_map/all_gather | solution.py:52
  152.2 9.2 %fusion.34 = bf16[3,1024,416]{1,2,0:T(8,128)(2,1)S(1)} fusion(f32[3,416]{1,0:T(4,128)S(1)} %copy-done.15, bf16[3,1664,416]{2,0,1:T(4,128)(2,1)} %all-gather.9.cloned.1.call-done, bf16[1024,1664]{1,0:T(8,128)(2,1)} %all-gather.7.cloned.1.call-done), kind=kOutput, calls=%fused_computation.53 | convolution fusion | flops 4255580160 | bytes 10122112 | tf_op jit(solution)/shard_map/td,cde->cte/dot_general | solution.py:49
  161.4 1.4 fusion.96
  162.8 0.6 reshape_squeeze.10
  163.4 1.0 copy.34
  164.4 15.8 %while.10 = (s32[]{:T(128)}, bf16[2,512,4,104]{1,3,2,0:T(8,128)(2,1)}, s32[2,512]{1,0:T(2,128)S(1)}, s32[1,1024]{1,0:T(1,128)S(1)}, bf16[2,512,4,104]{1,3,2,0:T(...) while((s32[]{:T(128)}, bf16[2,512,4,104]{1,3,2,0:T(8,128)(2,1)}, ...), condition=%wide.region_8.9_spmd, body=%wide.region_6.8_spmd.sunk | while | flops 887830528 | bytes 31156912 | solution.py:78
  164.4 0.4 broadcast_compare_fusion.2
  164.8 4.0 fusion.112
  168.8 2.5 fusion.113
  171.3 0.9 copy-done.6
  172.3 0.4 broadcast_compare_fusion.2
  172.6 4.0 fusion.112
  176.6 2.5 fusion.113
  179.2 0.9 copy-done.6
  180.2 2.0 copy.35
  182.2 0.2 copy.40
  182.4 3.9 convolution_convert_fusion
  186.4 0.0 all-gather.11.cloned.1.call-start
  186.4 38.9 %reduce-scatter.2.cloned.1.call-done = bf16[256,1664]{1,0:T(8,128)(2,1)} async-done(((bf16[1024,1664]{1,0:T(8,128)(2,1)}), bf16[256,1664]{1,0:T(8,128)(2,1)}) %reduce-scatter.2.cloned.1.call-update) | async-done | bytes 851984 | tf_op jit(solution)/shard_map/reduce_scatter | solution.py:80
  225.3 1.5 fusion.57
  226.9 1.7 multiply_reduce_fusion
  228.5 2.6 add_convert_fusion.2
  231.2 0.0 all-reduce.2.cloned.1.call-start
  231.3 41.5 %all-gather.11.cloned.1.call-done = bf16[1024,1664]{1,0:T(8,128)(2,1)} async-done(((bf16[256,1664]{1,0:T(8,128)(2,1)}), bf16[1024,1664]{1,0:T(8,128)(2,1)}) %all-gather.11.cloned.1.call-update) | async-done | bytes 3407888 | tf_op jit(solution)/shard_map/all_gather | solution.py:90
  272.7 11.1 %fusion.97 = f32[1024,2048]{1,0:T(8,128)S(1)} fusion(bf16[1024,1664]{1,0:T(8,128)(2,1)} %all-gather.11.cloned.1.call-done, bf16[1664,2048]{1,0:T(8,128)(2,1)} %param.34), kind=kOutput, calls=%fused_computation.133 | convolution fusion | flops 6979321856 | bytes 18612224 | tf_op jit(solution)/shard_map/dot_general | solution.py:89
  283.9 28.8 %fusion.29 = f32[1024,1664]{1,0:T(8,128)S(1)} fusion(bf16[2048,1664]{1,0:T(8,128)(2,1)} %param.36, f32[1024,2048]{1,0:T(8,128)S(1)} %fusion.97, f32[2048]{0:T(1024)S(1)} %copy-done.16), kind=kOutput, calls=%fused_computation.48 | convolution fusion | flops 7117733888 | bytes 22028288 | tf_op jit(solution)/shard_map/dot_general | solution.py:97
  312.8 0.4 add_dynamic-update-slice_fusion
  313.2 2.2 convert_element_type.78
  315.4 0.0 all-gather.13.cloned.1.call-start
  315.5 0.7 all-gather.13.cloned.1.call-update
  316.2 0.1 copy.36
  316.4 0.1 reshape_squeeze.11
  316.5 1.4 gather_fusion
  317.9 0.1 select_reduce_fusion
  318.0 0.6 reduce-window.6
  318.6 0.2 slice_reduce_fusion
  318.8 0.2 copy.31
  319.0 0.9 broadcast_in_dim.40
  320.0 2.0 copy.39
  322.0 0.1 fusion.62
  322.1 73.7 %all-reduce.2.cloned.1.call-done = bf16[1024,1664]{1,0:T(8,128)(2,1)} async-done(((bf16[1024,1664]{1,0:T(8,128)(2,1)}), bf16[1024,1664]{1,0:T(8,128)(2,1)}) %all-reduce.2.cloned.1.call-update) | async-done | bytes 3407888 | tf_op jit(solution)/shard_map/psum | solution.py:101
  395.8 2.8 convert_reduce_fusion
  398.7 3.2 fusion.23
  401.9 1.8 fusion.26
  403.7 5.9 %gather_fusion.1 = bf16[1024,1664]{1,0:T(8,128)(2,1)} fusion(bf16[1024,1664]{1,0:T(8,128)(2,1)S(1)} %fusion.26, s32[1024]{0:T(1024)S(1)} %broadcast_clamp_fusion), kind=kCustom, calls=%fused_computation.1 | custom fusion | bytes 6819840 | tf_op jit(solution)/shard_map/jit(_take)/gather | solution.py:106
  409.6 5.4 %gather.15 = bf16[256,6656]{1,0:T(8,128)(2,1)S(1)} reshape(bf16[1024,1664]{1,0:T(8,128)(2,1)} %gather_fusion.1) | data formatting | bytes 6815744 | tf_op jit(solution)/shard_map/jit(_take)/gather | solution.py:106
  415.0 33.5 %all-gather.13.cloned.1.call-done = bf16[6656,416]{1,0:T(8,128)(2,1)} async-done(((bf16[208,416]{1,0:T(8,128)(2,1)}), bf16[6656,416]{1,0:T(8,128)(2,1)}) %all-gather.13.cloned.1.call-update) | async-done | bytes 5537808 | tf_op jit(solution)/shard_map/all_gather | solution.py:112
  448.5 7.0 %convolution_convert_fusion.1 = bf16[512,416]{0,1:T(8,128)(2,1)} fusion(bf16[6656,416]{1,0:T(8,128)(2,1)} %all-gather.13.cloned.1.call-done, pred[256,6656]{1,0:T(8,128)(4,1)} %bitcast.118, bf16[256,6656]{1,0:T(8,128)(2,1)S(1)} %gather.15, s32[256]{0:T(256)S(1)} %multiply_add_fusion, f32[416]{0:T(512)S(1)} %copy-done.17), kind=kOutput, calls=%fused_computation.69 | convolution fusion | flops 1528987648 | bytes 11078272 | tf_op jit(solution)/shard_map/dot_general | solution.py:133
  455.5 1.2 copy.37
  456.7 16.2 %all_to_all.5 = bf16[32,16,416]{2,1,0:T(8,128)(2,1)S(1)} all-to-all(bf16[32,16,416]{2,1,0:T(8,128)(2,1)S(1)} %bitcast.116), channel_id=1, replica_groups=mesh['blk'=4,'tok'=32] {'tok'}, dimensions={0} | all-to-all | bytes 851968 | tf_op jit(solution)/shard_map/all_to_all | solution.py:135
  472.9 0.8 copy.56
  (66 shorter events, 0.3 us)
Async XLA Ops:
  6.5 145.7 %copy-start.15 = (f32[3,416]{1,0:T(4,128)S(1)}, f32[3,416]{1,0:T(4,128)}, u32[]{:S(2)}) copy-start(f32[3,416]{1,0:T(4,128)} %param.29) | copy-start | bytes 14980
  6.5 50.4 %all-gather.15.cloned.1.call-start = ((), (), s32[]{:S(2)}) async-start(), calls=%async_computation.8 | async-start | bytes 1892352 | tf_op jit(solution)/shard_map/all_gather | solution.py:79
  7.3 91.8 %all-gather.7.cloned.1.call-start = ((), (), s32[]{:S(2)}) async-start(), calls=%async_computation.2 | async-start | bytes 4259840 | tf_op jit(solution)/shard_map/all_gather | solution.py:46
  12.8 139.4 %all-gather.9.cloned.1.call-start = ((), (), s32[]{:S(2)}) async-start(), calls=%async_computation.3 | async-start | bytes 7028736 | tf_op jit(solution)/shard_map/all_gather | solution.py:52
  14.5 210.8 %reduce-scatter.2.cloned.1.call-start = ((), (), s32[]{:S(2)}) async-start(), calls=%async_computation.4 | async-start | bytes 4259840 | tf_op jit(solution)/shard_map/reduce_scatter | solution.py:80
  161.4 3.0 copy-start
  164.4 4.3 copy-start.4
  164.4 4.3 copy-start.5
  171.3 0.9 copy-start.6
  172.2 4.3 copy-start.4
  172.2 4.3 copy-start.5
  179.1 0.9 copy-start.6
  182.4 42.9 %copy-start.1 = (bf16[1,256,1664]{2,1,0:T(8,128)(2,1)S(1)}, bf16[1,256,1664]{2,1,0:T(8,128)(2,1)}, u32[]{:S(2)}) copy-start(bf16[1,256,1664]{2,1,0:T(8,128)(2,1)} %param.22) | copy-start | bytes 2555908
  182.4 42.9 %copy-start.7 = (f32[1664]{0:T(1024)S(1)}, f32[1664]{0:T(1024)}, u32[]{:S(2)}) copy-start(f32[1664]{0:T(1024)} %param.31) | copy-start | bytes 19972
  186.4 42.2 %copy-start.10 = (f32[1664]{0:T(1024)S(1)}, f32[1664]{0:T(1024)}, u32[]{:S(2)}) copy-start(f32[1664]{0:T(1024)} %param.33) | copy-start | bytes 19972
  186.4 42.2 %copy-start.11 = (f32[1664]{0:T(1024)S(1)}, f32[1664]{0:T(1024)}, u32[]{:S(2)}) copy-start(f32[1664]{0:T(1024)} %param.32) | copy-start | bytes 19972
  186.4 86.3 %all-gather.11.cloned.1.call-start = ((), (), s32[]{:S(2)}) async-start(), calls=%async_computation.5 | async-start | bytes 4259840 | tf_op jit(solution)/shard_map/all_gather | solution.py:90
  231.2 164.6 %all-reduce.2.cloned.1.call-start = ((), (), s32[]{:S(2)}) async-start(), calls=%async_computation.6 | async-start | bytes 6815744 | tf_op jit(solution)/shard_map/psum | solution.py:101
  231.2 52.6 %copy-start.16 = (f32[2048]{0:T(1024)S(1)}, f32[2048]{0:T(1024)}, u32[]{:S(2)}) copy-start(f32[2048]{0:T(1024)} %param.35) | copy-start | bytes 24580
  283.9 28.9 %copy-start.3 = (bf16[256,1664]{1,0:T(8,128)(2,1)S(1)}, bf16[256,1664]{1,0:T(8,128)(2,1)}, u32[]{:S(2)}) copy-start(bf16[256,1664]{1,0:T(8,128)(2,1)} %reduce-scatter.2.cloned.1.call-done) | copy-start | bytes 2555908
  313.2 3.0 copy-start.9
  313.2 4.7 copy-start.14
  315.4 80.4 %copy-start.8 = (f32[1664]{0:T(1024)S(1)}, f32[1664]{0:T(1024)}, u32[]{:S(2)}) copy-start(f32[1664]{0:T(1024)} %param.37) | copy-start | bytes 19972
  315.4 133.1 %all-gather.13.cloned.1.call-start = ((), (), s32[]{:S(2)}) async-start(), calls=%async_computation.7 | async-start | bytes 7028736 | tf_op jit(solution)/shard_map/all_gather | solution.py:112
  316.2 85.7 %copy-start.12 = (f32[1664]{0:T(1024)S(1)}, f32[1664]{0:T(1024)}, u32[]{:S(2)}) copy-start(f32[1664]{0:T(1024)} %param.39) | copy-start | bytes 19972
  316.2 85.6 %copy-start.13 = (f32[1664]{0:T(1024)S(1)}, f32[1664]{0:T(1024)}, u32[]{:S(2)}) copy-start(f32[1664]{0:T(1024)} %param.38) | copy-start | bytes 19972
  395.8 6.1 %copy-start.2 = (bf16[1024,1664]{1,0:T(8,128)(2,1)S(1)}, bf16[1024,1664]{1,0:T(8,128)(2,1)}, u32[]{:S(2)}) copy-start(bf16[1024,1664]{1,0:T(8,128)(2,1)} %all-reduce.2.cloned.1.call-done) | copy-start | bytes 10223620
  409.6 39.0 %copy-start.17 = (f32[416]{0:T(512)S(1)}, f32[416]{0:T(512)}, u32[]{:S(2)}) copy-start(f32[416]{0:T(512)} %param.41) | copy-start | bytes 4996
Sparse Core Ops, SparseCore 0:
  9.6 47.2 all-gather.14
  58.6 40.4 all-gather.6
  101.3 50.8 all-gather.8
  186.5 38.7 reduce-scatter.1
  231.3 41.3 all-gather.10
  315.5 80.1 all-reduce.1
  398.0 50.4 all-gather.12
where the time goes:
time: 490 us; the launch traced here: 481 us
  waiting for transfers between devices  322 us (66%)
  matrix products  73 us (15%)
  local copies, waits for them, and re-layouts  30.3 us (6%)
  other arithmetic  24.6 us (5%)
  blocking collectives  16.2 us (3%)
  between operations  14 us (3%)
    psum x1, waiting for transfers between devices, body(): lax.psum(partial_sum.astype(jnp.bfloat16), 'blk').astype(jnp.float32)  73.7 us
    all_gather x1, waiting for transfers between devices, body(): lax.all_gather(w_qkv, 'tok', axis=1, tiled=True)  53.1 us
    all_gather x1, waiting for transfers between devices, body(): lax.all_gather(normed_two, 'blk', axis=0, tiled=True)  41.5 us
    all_gather x1, waiting for transfers between devices, body(): out_full = lax.all_gather(w_out, 'tok', axis=1, tiled=True)  40.5 us
    all_gather x1, waiting for transfers between devices, body(): normed_all = lax.all_gather(normed_one, 'blk', axis=0, tiled=True)  39.4 us
    reduce_scatter x1, waiting for transfers between devices, body(): lax.psum_scatter(jnp.dot(attended, out_full, preferred_element_type=jnp.f...  38.9 us
    all_gather x1, waiting for transfers between devices, body(): lax.all_gather(w_proj, 'tok', axis=0, tiled=True)  33.5 us
    dot_general x1, matrix products, body(): partial_sum = jnp.dot(hidden_act, w_fc2, preferred_element_type=jnp.float32)  28.8 us
  transfers between devices with their start and end apart: 7, of which 7 were waited for; matrix products, arithmetic and copies ran while one was open for 8% of the time, Pallas kernels for 0%

commit v1 on v0

--- a/solution.py
+++ b/solution.py
@@ -98,7 +98,9 @@
     own_start = lax.axis_index("blk") * row_count
     own_rows = lax.dynamic_slice_in_dim(partial_sum, own_start, row_count, 0) + after_attn
     partial_sum = lax.dynamic_update_slice_in_dim(partial_sum, own_rows, own_start, 0)
-    summed = lax.psum(partial_sum.astype(jnp.bfloat16), "blk").astype(jnp.float32)
+    summed = jnp.sum(lax.all_gather(partial_sum.astype(jnp.bfloat16), "blk"), axis=0).astype(
+        jnp.float32
+    )
     layer_all = (summed + fc2_bias).astype(jnp.bfloat16)
     final_all = layer_norm(layer_all, ln3_gain, ln3_bias).astype(jnp.bfloat16)
     merge_rows = merge_index[0]

time: 490 us -> 539 us (1.10)
  waiting for transfers between devices: 322 us -> 364 us
  other arithmetic: 24.6 us -> 31 us
    all_gather x0 -> x1, waiting for transfers between devices: none -> 121 us  [body(): lax.all_gather(partial_sum.astype(jnp.bfloat16), 'blk')]
    psum x1 -> x0, waiting for transfers between devices: 73.7 us -> none  [body(): lax.psum(partial_sum.astype(jnp.bfloat16), 'blk').astype(jnp.float32)]
    reduce_sum x0 -> x1, other arithmetic: none -> 9.18 us  [body(): jnp.sum(lax.all_gather(partial_sum.astype(jnp.bfloat16), 'blk'), axis=0)]
    all_gather x1, waiting for transfers between devices: 33.5 us -> 27.9 us  [body(): lax.all_gather(w_proj, 'tok', axis=0, tiled=True)]
where the time goes in v1:
time: 539 us; the launch traced here: 530 us
  waiting for transfers between devices  364 us (68%)
  matrix products  73 us (14%)
  other arithmetic  31 us (6%)
  local copies, waits for them, and re-layouts  30.6 us (6%)
  blocking collectives  16.2 us (3%)
  between operations  14.3 us (3%)
    all_gather x1, waiting for transfers between devices, body(): lax.all_gather(partial_sum.astype(jnp.bfloat16), 'blk')  121 us
    all_gather x1, waiting for transfers between devices, body(): lax.all_gather(w_qkv, 'tok', axis=1, tiled=True)  53.1 us
    all_gather x1, waiting for transfers between devices, body(): lax.all_gather(normed_two, 'blk', axis=0, tiled=True)  41.5 us
    all_gather x1, waiting for transfers between devices, body(): out_full = lax.all_gather(w_out, 'tok', axis=1, tiled=True)  40.5 us
    all_gather x1, waiting for transfers between devices, body(): normed_all = lax.all_gather(normed_one, 'blk', axis=0, tiled=True)  39.4 us
    reduce_scatter x1, waiting for transfers between devices, body(): lax.psum_scatter(jnp.dot(attended, out_full, preferred_element_type=jnp.f...  38.9 us
    dot_general x1, matrix products, body(): partial_sum = jnp.dot(hidden_act, w_fc2, preferred_element_type=jnp.float32)  28.6 us
    all_gather x1, waiting for transfers between devices, body(): lax.all_gather(w_proj, 'tok', axis=0, tiled=True)  27.9 us
  transfers between devices with their start and end apart: 7, of which 7 were waited for; matrix products, arithmetic and copies ran while one was open for 8% of the time, Pallas kernels for 0%

profile of v1, /device:TPU:1, one launch (start us, length us, event | category | flops | bytes accessed | tf_op | source)
XLA Modules:
  0.0 529.6 jit_solution(2551173348352485808)
XLA Ops:
  6.5 0.7 all-gather.19.cloned.1.call-update
  7.3 1.3 convert_reduce_fusion.1
  8.7 1.5 fusion.43
  10.2 2.5 fusion.46
  12.8 0.0 all-gather.11.cloned.1.call-start
  12.8 1.7 copy.32
  14.5 0.0 reduce-scatter.2.cloned.1.call-start
  14.6 0.5 broadcast.197
  15.1 1.3 reduce.7
  16.4 40.5 %all-gather.19.cloned.1.call-done = bf16[32,52,416]{2,1,0:T(8,128)(2,1)} async-done(((bf16[1,52,416]{2,1,0:T(8,128)(2,1)}), bf16[32,52,416]{2,1,0:T(8,128)(2,1)}) %all-gather.19.cloned.1.call-update) | async-done | bytes 1384464 | tf_op jit(solution)/shard_map/all_gather | solution.py:79
  56.9 2.7 reshape.180
  59.7 39.4 %all-gather.9.cloned.1.call-done = bf16[1024,1664]{1,0:T(8,128)(2,1)} async-done(((bf16[256,1664]{1,0:T(8,128)(2,1)}), bf16[1024,1664]{1,0:T(8,128)(2,1)}) %all-gather.9.cloned.1.call-update) | async-done | bytes 3407888 | tf_op jit(solution)/shard_map/all_gather | solution.py:46
  99.1 53.1 %all-gather.11.cloned.1.call-done = bf16[3,1664,416]{2,0,1:T(4,128)(2,1)} async-done(((bf16[3,52,416]{2,0,1:T(4,128)(2,1)}), bf16[3,1664,416]{2,0,1:T(4,128)(2,1)}) %all-gather.11.cloned.1.call-update) | async-done | bytes 4153360 | tf_op jit(solution)/shard_map/all_gather | solution.py:52
  152.2 9.2 %fusion.34 = bf16[3,1024,416]{1,2,0:T(8,128)(2,1)S(1)} fusion(f32[3,416]{1,0:T(4,128)S(1)} %copy-done.15, bf16[3,1664,416]{2,0,1:T(4,128)(2,1)} %all-gather.11.cloned.1.call-done, bf16[1024,1664]{1,0:T(8,128)(2,1)} %all-gather.9.cloned.1.call-done), kind=kOutput, calls=%fused_computation.53 | convolution fusion | flops 4255580160 | bytes 10122112 | tf_op jit(solution)/shard_map/td,cde->cte/dot_general | solution.py:49
  161.4 1.4 fusion.96
  162.8 0.6 reshape_squeeze.10
  163.4 1.0 copy.34
  164.4 15.8 %while.10 = (s32[]{:T(128)}, bf16[2,512,4,104]{1,3,2,0:T(8,128)(2,1)}, s32[2,512]{1,0:T(2,128)S(1)}, s32[1,1024]{1,0:T(1,128)S(1)}, bf16[2,512,4,104]{1,3,2,0:T(...) while((s32[]{:T(128)}, bf16[2,512,4,104]{1,3,2,0:T(8,128)(2,1)}, ...), condition=%wide.region_8.9_spmd, body=%wide.region_6.8_spmd.sunk | while | flops 887830528 | bytes 31156912 | solution.py:78
  164.4 0.4 broadcast_compare_fusion.2
  164.8 3.9 fusion.112
  168.8 2.5 fusion.113
  171.3 0.9 copy-done.6
  172.3 0.4 broadcast_compare_fusion.2
  172.6 4.0 fusion.112
  176.6 2.5 fusion.113
  179.1 0.9 copy-done.6
  180.2 2.0 copy.35
  182.3 0.2 copy.40
  182.5 3.9 convolution_convert_fusion
  186.4 0.0 all-gather.13.cloned.1.call-start
  186.5 38.9 %reduce-scatter.2.cloned.1.call-done = bf16[256,1664]{1,0:T(8,128)(2,1)} async-done(((bf16[1024,1664]{1,0:T(8,128)(2,1)}), bf16[256,1664]{1,0:T(8,128)(2,1)}) %reduce-scatter.2.cloned.1.call-update) | async-done | bytes 851984 | tf_op jit(solution)/shard_map/reduce_scatter | solution.py:80
  225.4 1.5 fusion.57
  226.9 1.7 multiply_reduce_fusion
  228.6 2.6 add_convert_fusion.2
  231.2 0.0 all-gather.17.cloned.1.call-start
  231.3 41.5 %all-gather.13.cloned.1.call-done = bf16[1024,1664]{1,0:T(8,128)(2,1)} async-done(((bf16[256,1664]{1,0:T(8,128)(2,1)}), bf16[1024,1664]{1,0:T(8,128)(2,1)}) %all-gather.13.cloned.1.call-update) | async-done | bytes 3407888 | tf_op jit(solution)/shard_map/all_gather | solution.py:90
  272.8 11.3 %fusion.97 = f32[1024,2048]{1,0:T(8,128)S(1)} fusion(bf16[1024,1664]{1,0:T(8,128)(2,1)} %all-gather.13.cloned.1.call-done, bf16[1664,2048]{1,0:T(8,128)(2,1)} %param.34), kind=kOutput, calls=%fused_computation.133 | convolution fusion | flops 6979321856 | bytes 18612224 | tf_op jit(solution)/shard_map/dot_general | solution.py:89
  284.1 28.6 %fusion.29 = f32[1024,1664]{1,0:T(8,128)S(1)} fusion(bf16[2048,1664]{1,0:T(8,128)(2,1)} %param.36, f32[1024,2048]{1,0:T(8,128)S(1)} %fusion.97, f32[2048]{0:T(1024)S(1)} %copy-done.16), kind=kOutput, calls=%fused_computation.48 | convolution fusion | flops 7117733888 | bytes 22028288 | tf_op jit(solution)/shard_map/dot_general | solution.py:97
  312.8 0.4 add_dynamic-update-slice_fusion
  313.3 2.1 convert_element_type.80
  315.4 0.0 all-gather.15.cloned.1.call-start
  315.4 0.7 all-gather.15.cloned.1.call-update
  316.2 0.1 copy.36
  316.3 0.1 reshape_squeeze.11
  316.4 1.4 gather_fusion
  317.8 0.1 select_reduce_fusion
  317.9 0.6 reduce-window.6
  318.5 0.2 slice_reduce_fusion
  318.8 0.2 copy.31
  319.0 0.9 broadcast_in_dim.40
  319.9 2.1 copy.39
  322.0 0.1 fusion.62
  322.1 121.1 %all-gather.17.cloned.1.call-done = bf16[4096,1664]{1,0:T(8,128)(2,1)} async-done(((bf16[1024,1664]{1,0:T(8,128)(2,1)}), bf16[4096,1664]{1,0:T(8,128)(2,1)}) %all-gather.17.cloned.1.call-update) | async-done | bytes 13631504 | tf_op jit(solution)/shard_map/all_gather | solution.py:101
  443.3 9.2 %reduce_sum.99 = bf16[1024,1664]{1,0:T(8,128)(2,1)S(1)} reduce(bf16[4,1024,1664]{2,1,0:T(8,128)(2,1)} %bitcast.115, bf16[]{:T(256)} %constant.57.clone.1), dimensions={0}, to_apply=%region_12.13 | reduce | flops 5111808 | bytes 17039362 | tf_op jit(solution)/shard_map/reduce_sum | solution.py:101
  452.5 0.7 convert_reduce_fusion
  453.2 1.2 fusion.23
  454.5 3.2 fusion.26
  457.7 5.8 %gather_fusion.1 = bf16[1024,1664]{1,0:T(8,128)(2,1)} fusion(bf16[1024,1664]{1,0:T(8,128)(2,1)S(1)} %fusion.26, s32[1024]{0:T(1024)S(1)} %broadcast_clamp_fusion), kind=kCustom, calls=%fused_computation.1 | custom fusion | bytes 6819840 | tf_op jit(solution)/shard_map/jit(_take)/gather | solution.py:108
  463.5 5.7 %gather.15 = bf16[256,6656]{1,0:T(8,128)(2,1)S(1)} reshape(bf16[1024,1664]{1,0:T(8,128)(2,1)} %gather_fusion.1) | data formatting | bytes 6815744 | tf_op jit(solution)/shard_map/jit(_take)/gather | solution.py:108
  469.2 27.9 %all-gather.15.cloned.1.call-done = bf16[6656,416]{1,0:T(8,128)(2,1)} async-done(((bf16[208,416]{1,0:T(8,128)(2,1)}), bf16[6656,416]{1,0:T(8,128)(2,1)}) %all-gather.15.cloned.1.call-update) | async-done | bytes 5537808 | tf_op jit(solution)/shard_map/all_gather | solution.py:114
  497.1 7.0 %convolution_convert_fusion.1 = bf16[512,416]{0,1:T(8,128)(2,1)} fusion(bf16[6656,416]{1,0:T(8,128)(2,1)} %all-gather.15.cloned.1.call-done, pred[256,6656]{1,0:T(8,128)(4,1)} %bitcast.120, bf16[256,6656]{1,0:T(8,128)(2,1)S(1)} %gather.15, s32[256]{0:T(256)S(1)} %multiply_add_fusion, f32[416]{0:T(512)S(1)} %copy-done.17), kind=kOutput, calls=%fused_computation.69 | convolution fusion | flops 1528987648 | bytes 11078272 | tf_op jit(solution)/shard_map/dot_general | solution.py:135
  504.1 1.2 copy.37
  505.3 16.2 %all_to_all.5 = bf16[32,16,416]{2,1,0:T(8,128)(2,1)S(1)} all-to-all(bf16[32,16,416]{2,1,0:T(8,128)(2,1)S(1)} %bitcast.118), channel_id=1, replica_groups=mesh['blk'=4,'tok'=32] {'tok'}, dimensions={0} | all-to-all | bytes 851968 | tf_op jit(solution)/shard_map/all_to_all | solution.py:137
  521.5 0.8 copy.55
  (67 shorter events, 0.4 us)
Async XLA Ops:
  6.5 145.7 %copy-start.15 = (f32[3,416]{1,0:T(4,128)S(1)}, f32[3,416]{1,0:T(4,128)}, u32[]{:S(2)}) copy-start(f32[3,416]{1,0:T(4,128)} %param.29) | copy-start | bytes 14980
  6.5 50.4 %all-gather.19.cloned.1.call-start = ((), (), s32[]{:S(2)}) async-start(), calls=%async_computation.8 | async-start | bytes 1892352 | tf_op jit(solution)/shard_map/all_gather | solution.py:79
  7.3 91.8 %all-gather.9.cloned.1.call-start = ((), (), s32[]{:S(2)}) async-start(), calls=%async_computation.2 | async-start | bytes 4259840 | tf_op jit(solution)/shard_map/all_gather | solution.py:46
  12.8 139.4 %all-gather.11.cloned.1.call-start = ((), (), s32[]{:S(2)}) async-start(), calls=%async_computation.3 | async-start | bytes 7028736 | tf_op jit(solution)/shard_map/all_gather | solution.py:52
  14.5 210.8 %reduce-scatter.2.cloned.1.call-start = ((), (), s32[]{:S(2)}) async-start(), calls=%async_computation.4 | async-start | bytes 4259840 | tf_op jit(solution)/shard_map/reduce_scatter | solution.py:80
  161.4 3.0 copy-start
  164.4 4.3 copy-start.4
  164.4 4.3 copy-start.5
  171.3 0.9 copy-start.6
  172.2 4.3 copy-start.4
  172.2 4.3 copy-start.5
  179.1 0.9 copy-start.6
  182.5 42.9 %copy-start.2 = (bf16[1,256,1664]{2,1,0:T(8,128)(2,1)S(1)}, bf16[1,256,1664]{2,1,0:T(8,128)(2,1)}, u32[]{:S(2)}) copy-start(bf16[1,256,1664]{2,1,0:T(8,128)(2,1)} %param.22) | copy-start | bytes 2555908
  182.5 42.9 %copy-start.7 = (f32[1664]{0:T(1024)S(1)}, f32[1664]{0:T(1024)}, u32[]{:S(2)}) copy-start(f32[1664]{0:T(1024)} %param.31) | copy-start | bytes 19972
  186.4 42.2 %copy-start.10 = (f32[1664]{0:T(1024)S(1)}, f32[1664]{0:T(1024)}, u32[]{:S(2)}) copy-start(f32[1664]{0:T(1024)} %param.33) | copy-start | bytes 19972
  186.4 42.2 %copy-start.11 = (f32[1664]{0:T(1024)S(1)}, f32[1664]{0:T(1024)}, u32[]{:S(2)}) copy-start(f32[1664]{0:T(1024)} %param.32) | copy-start | bytes 19972
  186.4 86.3 %all-gather.13.cloned.1.call-start = ((), (), s32[]{:S(2)}) async-start(), calls=%async_computation.5 | async-start | bytes 4259840 | tf_op jit(solution)/shard_map/all_gather | solution.py:90
  231.2 212.0 %all-gather.17.cloned.1.call-start = ((), (), s32[]{:S(2)}) async-start(), calls=%async_computation.7 | async-start | bytes 17039360 | tf_op jit(solution)/shard_map/all_gather | solution.py:101
  231.3 52.8 %copy-start.16 = (f32[2048]{0:T(1024)S(1)}, f32[2048]{0:T(1024)}, u32[]{:S(2)}) copy-start(f32[2048]{0:T(1024)} %param.35) | copy-start | bytes 24580
  284.1 28.7 %copy-start.3 = (bf16[256,1664]{1,0:T(8,128)(2,1)S(1)}, bf16[256,1664]{1,0:T(8,128)(2,1)}, u32[]{:S(2)}) copy-start(bf16[256,1664]{1,0:T(8,128)(2,1)} %reduce-scatter.2.cloned.1.call-done) | copy-start | bytes 2555908
  313.2 2.9 copy-start.9
  313.3 4.6 copy-start.14
  315.4 181.7 %all-gather.15.cloned.1.call-start = ((), (), s32[]{:S(2)}) async-start(), calls=%async_computation.6 | async-start | bytes 7028736 | tf_op jit(solution)/shard_map/all_gather | solution.py:114
  443.3 9.2 %copy-start.8 = (f32[1664]{0:T(1024)S(1)}, f32[1664]{0:T(1024)}, u32[]{:S(2)}) copy-start(f32[1664]{0:T(1024)} %param.37) | copy-start | bytes 19972
  452.5 2.0 copy-start.1
  452.5 2.0 copy-start.12
  452.5 2.0 copy-start.13
  463.5 33.6 %copy-start.17 = (f32[416]{0:T(512)S(1)}, f32[416]{0:T(512)}, u32[]{:S(2)}) copy-start(f32[416]{0:T(512)} %param.41) | copy-start | bytes 4996
Sparse Core Ops, SparseCore 0:
  9.6 47.2 all-gather.18
  58.6 40.4 all-gather.8
  101.3 50.8 all-gather.10
  186.6 38.7 reduce-scatter.1
  231.3 41.3 all-gather.12
  315.5 127.6 all-gather.16
  445.5 51.5 all-gather.14
